TPU v7x, 32 devices: a whole 2x2x4 slice. The times are simulated.
32 devices in a mesh: depth: 2 (over core), lat: 16 (over z, y, x).
Axes of the slice: x: 2, y: 2, z: 4, core: 2. Of those that a mesh axis runs over, the one named last changes fastest.
Arguments:
- fields: float32 [6, 96, 16, 512], P(None, 'lat', 'depth'), may hold values from -3 to 3
- material: int32 [96, 16, 512], P('lat', 'depth'), may hold values from 0 to 3
- source_mask: int32 [96, 16, 512], P('lat', 'depth'), may hold values 0 or 1
- eps_table: float32 [4], replicated, may hold values from 1 to 6
- kerr_table: float32 [4], replicated, may hold values from 0.3 to 3
Outputs:
- fields_out: float32 [6, 96, 16, 512], P(None, 'lat', 'depth')
- image: float32 [96, 8, 512], P('lat', None, 'depth')
Inputs may be any that keep to these rules, and one draw needn't show every extreme that they name: material indexes the tables.
All inputs are finite; a program needn't handle non-finite values. No bound on the sum of `source_mask` on one device may be relied on, other than what follows from the above.
Results may differ from a plain program's by a relative error of at most 0.0003.
Values sent between devices are 32-bit elements; how exact they have to be, the bound alone decides.
No kernel may reach another device: no remote copies, remote signals or barrier semaphores. Data moves between devices by JAX's collectives and lax.ppermute only.
A program may use at most 64 MiB of HBM per device.

v0:
```python
import math
import jax
import jax.numpy as jnp
from jax import lax
from jax.sharding import PartitionSpec as P

STEPS = 16
HALO_STEPS = 4
COURANT = 0.55
OMEGAS = (0.9, 1.3)
SOURCE_AMP = 1.0
QUARTERS = (3, 5)
HIGHEST = lax.Precision.HIGHEST


def padded_2(block, sides, width):
    for axis, dim in sides:
        count = lax.axis_size(axis)
        forward = [(i, i + 1) for i in range(count - 1)]
        backward = [(target, source) for source, target in forward]
        low = lax.ppermute(
            lax.slice_in_dim(block, block.shape[dim] - width, None, axis=dim), axis, forward
        )
        high = lax.ppermute(lax.slice_in_dim(block, 0, width, axis=dim), axis, backward)
        block = jnp.concatenate([low, block, high], axis=dim)
    return block


def from_root(block, axis, owner):
    block = jnp.where(lax.axis_index(axis) == owner, block, jnp.zeros_like(block))
    return lax.psum(block, axis)


def forward_diff(field, along):
    length = field.shape[along]
    ahead = lax.slice_in_dim(field, 1, length, axis=along)
    ahead = jnp.concatenate(
        [ahead, jnp.zeros_like(lax.slice_in_dim(field, 0, 1, axis=along))], axis=along
    )
    return ahead - field


def backward_diff(field, along):
    length = field.shape[along]
    behind = lax.slice_in_dim(field, 0, length - 1, axis=along)
    behind = jnp.concatenate(
        [jnp.zeros_like(lax.slice_in_dim(field, 0, 1, axis=along)), behind], axis=along
    )
    return field - behind


def drive(moment):
    middle = moment + 0.5
    return SOURCE_AMP * (jnp.sin(OMEGAS[0] * middle) + jnp.sin(OMEGAS[1] * middle))


def yee_step(fields, permittivity, kerr_coef, source_flag, inside, pulse):
    elec_x, elec_y, elec_z = (fields[0], fields[1], fields[2])
    magn_x, magn_y, magn_z = (fields[3], fields[4], fields[5])
    magn_x = (magn_x - COURANT * (forward_diff(elec_z, 2) - forward_diff(elec_y, 1))) * inside
    magn_y = (magn_y - COURANT * (forward_diff(elec_x, 1) - forward_diff(elec_z, 0))) * inside
    magn_z = (magn_z - COURANT * (forward_diff(elec_y, 0) - forward_diff(elec_x, 2))) * inside
    energy = elec_x * elec_x + elec_y * elec_y + elec_z * elec_z
    factor = COURANT / (permittivity + kerr_coef * energy)
    new_x = (
        elec_x
        + factor * (backward_diff(magn_z, 2) - backward_diff(magn_y, 1))
        + source_flag * pulse
    ) * inside
    new_y = (elec_y + factor * (backward_diff(magn_x, 1) - backward_diff(magn_z, 0))) * inside
    new_z = (elec_z + factor * (backward_diff(magn_y, 0) - backward_diff(magn_x, 2))) * inside
    return jnp.stack([new_x, new_y, new_z, magn_x, magn_y, magn_z])


def lookup(material, table):
    result = jnp.zeros(material.shape, jnp.float32)
    for level in range(table.shape[0]):
        result = jnp.where(material == level, table[level], result)
    return result


def accumulate(spectrum, plane, moment):
    later = moment + 1.0
    trig = jnp.stack(
        [jnp.stack([jnp.cos(omega * later), -jnp.sin(omega * later)]) for omega in OMEGAS]
    )
    return spectrum + trig[:, None, :, None, None] * plane[None, :, None, :, :]


def chirp(row_index, col_index, length):
    gap = row_index[:, None] - col_index[None, :]
    squared = gap * gap
    reals, imags = ([], [])
    for quarter in QUARTERS:
        wrapped = quarter * squared % (8 * length)
        phase = wrapped.astype(jnp.float32) * (math.pi / (4.0 * length))
        reals.append(jnp.cos(phase) / math.sqrt(length))
        imags.append(jnp.sin(phase) / math.sqrt(length))
    return (jnp.stack(reals), jnp.stack(imags))


def column_transform(real, imag, y_real, y_imag):
    v_real = jnp.einsum("fcxy,fyk->fcxk", real, y_real, precision=HIGHEST) - jnp.einsum(
        "fcxy,fyk->fcxk", imag, y_imag, precision=HIGHEST
    )
    v_imag = jnp.einsum("fcxy,fyk->fcxk", real, y_imag, precision=HIGHEST) + jnp.einsum(
        "fcxy,fyk->fcxk", imag, y_real, precision=HIGHEST
    )
    return (v_real, v_imag)


def row_transform(x_real, x_imag, v_real, v_imag):
    w_real = jnp.einsum("fix,fcxk->ifck", x_real, v_real, precision=HIGHEST) - jnp.einsum(
        "fix,fcxk->ifck", x_imag, v_imag, precision=HIGHEST
    )
    w_imag = jnp.einsum("fix,fcxk->ifck", x_real, v_imag, precision=HIGHEST) + jnp.einsum(
        "fix,fcxk->ifck", x_imag, v_real, precision=HIGHEST
    )
    return jnp.stack([w_real, w_imag], axis=3)


def local(fields, material, source_mask, eps_table, kerr_table):
    width_x = fields.shape[1]
    depth_z = fields.shape[2]
    span_y = fields.shape[3]
    lat_count = lax.axis_size("lat")
    depth_count = lax.axis_size("depth")
    total_x = width_x * lat_count
    total_z = depth_z * depth_count
    lat_pos = lax.axis_index("lat")
    depth_pos = lax.axis_index("depth")
    coefs = jnp.stack(
        [lookup(material, eps_table), lookup(material, kerr_table), source_mask.astype(jnp.float32)]
    )
    empty_spectrum = jnp.zeros((2, 2, 2, width_x, span_y), jnp.float32)
    coef_pad = padded_2(coefs, (("depth", 2), ("lat", 1)), HALO_STEPS)
    place_x = lat_pos * width_x - HALO_STEPS + jnp.arange(width_x + 2 * HALO_STEPS, dtype=jnp.int32)
    place_z = (
        depth_pos * depth_z - HALO_STEPS + jnp.arange(depth_z + 2 * HALO_STEPS, dtype=jnp.int32)
    )
    valid_x = (place_x >= 0) & (place_x < total_x)
    valid_z = (place_z >= 0) & (place_z < total_z)
    valid = valid_x[:, None] & valid_z[None, :]
    setup_inside = valid.astype(jnp.float32)[:, :, None]
    setup_permittivity = jnp.where(valid[:, :, None], coef_pad[0], 1.0)
    kerr_coef = coef_pad[1]
    source_flag = coef_pad[2]

    def one_block(block, carry):
        state, spectrum = carry
        padded = padded_2(state, (("depth", 2), ("lat", 1)), HALO_STEPS)
        for inner in range(HALO_STEPS):
            moment = (block * HALO_STEPS + inner).astype(jnp.float32)
            padded = yee_step(
                padded, setup_permittivity, kerr_coef, source_flag, setup_inside, drive(moment)
            )
            plane = padded[0:2, HALO_STEPS : HALO_STEPS + width_x, HALO_STEPS + depth_z - 1, :]
            spectrum = accumulate(spectrum, plane, moment)
        state = padded[:, HALO_STEPS : HALO_STEPS + width_x, HALO_STEPS : HALO_STEPS + depth_z]
        return (state, spectrum)

    state, spectrum = lax.fori_loop(0, STEPS // HALO_STEPS, one_block, (fields, empty_spectrum))
    spectrum = from_root(spectrum, "depth", depth_count - 1)
    col_count = span_y // depth_count
    col_index = depth_pos * col_count + jnp.arange(col_count, dtype=jnp.int32)
    y_real, y_imag = chirp(jnp.arange(span_y, dtype=jnp.int32), col_index, span_y)
    v_real, v_imag = column_transform(spectrum[:, :, 0], spectrum[:, :, 1], y_real, y_imag)
    row_local = lat_pos * width_x + jnp.arange(width_x, dtype=jnp.int32)
    row_index = jnp.arange(width_x * lax.axis_size("lat"), dtype=jnp.int32)
    x_real, x_imag = chirp(row_index, row_local, total_x)
    image = lax.psum_scatter(
        row_transform(x_real, x_imag, v_real, v_imag), "lat", scatter_dimension=0, tiled=True
    )
    return (state, image.reshape(width_x, 8, col_count))


def solution(mesh):
    placed = (
        P(None, "lat", "depth", None),
        P("lat", "depth", None),
        P("lat", "depth", None),
        P(),
        P(),
    )
    return jax.shard_map(
        local,
        mesh=mesh,
        in_specs=placed,
        out_specs=(P(None, "lat", "depth", None), P("lat", None, "depth")),
        check_vma=False,
    )
```

profile of v0, /device:TPU:0, one launch (start us, length us, event | category | flops | bytes accessed | tf_op | source)
XLA Modules:
  0.0 429.3 jit_solution(4723124953728280105)
XLA Ops:
  7.2 1.5 fusion.47
  8.7 1.5 fusion.46
  10.1 0.9 convert_bitcast_fusion.1
  11.0 3.4 select_bitcast_fusion.1
  14.5 2.5 select_bitcast_fusion
  17.0 2.4 collective-permute-start.4
  19.4 1.3 collective-permute-start.5
  20.9 1.8 collective-permute-done.5
  22.9 4.2 collective-permute-start.6
  27.1 1.3 collective-permute-start.7
  29.0 5.1 %cosine_multiply_fusion.1 = (f32[1,512,256]{2,1,0:T(8,128)}, f32[1,512,256]{2,1,0:T(8,128)}, f32[1,512,256]{2,1,0:T(8,128)}, f32[1,512,256]{2,1,0:T(8,128)}) fusion(s32[256]{0:T(256)S(1)} %iota_add_fusion), kind=kLoop, calls=%fused_computation.100 | loop fusion | flops 4456448 | bytes 2098176 | tf_op jit(solution)/shard_map/div | solution.py:97
  34.1 10.1 %collective-permute-done.6 = f32[3,4,16,512]{3,2,1,0:T(8,128)S(1)} collective-permute-done((f32[3,4,16,512]{3,2,1,0:T(8,128)S(1)}, f32[3,4,16,512]{3,2,1,0:T(8,128)S(1)}, u32[]{:S(2)}, u32[]{:S(2)}) %collective-permute-start.6) | collective-permute-done | bytes 393248 | tf_op jit(solution)/shard_map/ppermute | solution.py:21
  44.2 1.9 collective-permute-done.7
  46.6 234.1 %while.16 = (s32[]{:T(128)}, f32[6,6,8,512]{3,2,1,0:T(8,128)S(1)}, f32[2,2,2,6,512]{4,3,2,1,0:T(8,128)S(1)}, f32[14,16,512]{2,1,0:T(8,128)S(1)}, f32[14,16,512]{...) while((s32[]{:T(128)}, f32[6,6,8,512]{3,2,1,0:T(8,128)S(1)}, ...), condition=%wide.region_1.2_spmd.clone, body=%wide.region_0.1_spmd.clone.sunk | while | flops 24691188 | bytes 132281024 | solution.py:162
  46.9 1.3 collective-permute-start
  48.2 3.1 collective-permute-start.1
  52.9 1.1 fusion.57
  54.0 1.3 collective-permute-start.2
  55.3 5.5 %collective-permute-start.3 = (f32[6,4,16,512]{3,2,1,0:T(8,128)S(1)}, f32[6,4,16,512]{3,2,1,0:T(8,128)}, u32[]{:S(2)}, u32[]{:S(2)}) collective-permute-start(f32[6,4,16,512]{3,2,1,0:T(8,128)S(1)} %get-tuple-element.357), channel_id=1, source_target_pairs={{0,1},{1,2},{2,3},{3,4},{4,5},{5,6},{6,7},{7,8},{8,9},{9,10},{10,1... | collective-permute-start | bytes 2359304 | tf_op jit(solution)/shard_map/while/body/eval_jaxpr/ppermute | solution.py:21
  61.6 15.0 %collective-permute-done.2 = f32[6,4,16,512]{3,2,1,0:T(8,128)} collective-permute-done((f32[6,4,16,512]{3,2,1,0:T(8,128)}, f32[6,4,16,512]{3,2,1,0:T(8,128)}, u32[]{:S(2)}, u32[]{:S(2)}) %collective-permute-start.2) | collective-permute-done | bytes 786464 | tf_op jit(solution)/shard_map/while/body/eval_jaxpr/ppermute | solution.py:24
  76.6 14.7 %collective-permute-done.3 = f32[6,4,16,512]{3,2,1,0:T(8,128)} collective-permute-done((f32[6,4,16,512]{3,2,1,0:T(8,128)S(1)}, f32[6,4,16,512]{3,2,1,0:T(8,128)}, u32[]{:S(2)}, u32[]{:S(2)}) %collective-permute-start.3) | collective-permute-done | bytes 786464 | tf_op jit(solution)/shard_map/while/body/eval_jaxpr/ppermute | solution.py:21
  91.3 1.8 pad_maximum_fusion.25
  94.2 0.7 add_multiply_fusion.15
  96.5 0.7 add_multiply_fusion.17
  98.8 0.7 add_multiply_fusion.19
  103.5 1.3 collective-permute-start
  104.8 3.1 collective-permute-start.1
  109.5 1.1 fusion.57
  110.6 1.3 collective-permute-start.2
  111.9 6.0 %collective-permute-start.3 = (f32[6,4,16,512]{3,2,1,0:T(8,128)S(1)}, f32[6,4,16,512]{3,2,1,0:T(8,128)}, u32[]{:S(2)}, u32[]{:S(2)}) collective-permute-start(f32[6,4,16,512]{3,2,1,0:T(8,128)S(1)} %get-tuple-element.357), channel_id=1, source_target_pairs={{0,1},{1,2},{2,3},{3,4},{4,5},{5,6},{6,7},{7,8},{8,9},{9,10},{10,1... | collective-permute-start | bytes 2359304 | tf_op jit(solution)/shard_map/while/body/eval_jaxpr/ppermute | solution.py:21
  118.9 15.0 %collective-permute-done.2 = f32[6,4,16,512]{3,2,1,0:T(8,128)} collective-permute-done((f32[6,4,16,512]{3,2,1,0:T(8,128)}, f32[6,4,16,512]{3,2,1,0:T(8,128)}, u32[]{:S(2)}, u32[]{:S(2)}) %collective-permute-start.2) | collective-permute-done | bytes 786464 | tf_op jit(solution)/shard_map/while/body/eval_jaxpr/ppermute | solution.py:24
  133.8 17.1 %collective-permute-done.3 = f32[6,4,16,512]{3,2,1,0:T(8,128)} collective-permute-done((f32[6,4,16,512]{3,2,1,0:T(8,128)S(1)}, f32[6,4,16,512]{3,2,1,0:T(8,128)}, u32[]{:S(2)}, u32[]{:S(2)}) %collective-permute-start.3) | collective-permute-done | bytes 786464 | tf_op jit(solution)/shard_map/while/body/eval_jaxpr/ppermute | solution.py:21
  151.0 1.8 pad_maximum_fusion.25
  153.8 0.7 add_multiply_fusion.15
  156.1 0.7 add_multiply_fusion.17
  158.5 0.7 add_multiply_fusion.19
  163.2 1.3 collective-permute-start
  164.5 3.1 collective-permute-start.1
  169.2 1.1 fusion.57
  170.3 1.3 collective-permute-start.2
  171.6 6.0 %collective-permute-start.3 = (f32[6,4,16,512]{3,2,1,0:T(8,128)S(1)}, f32[6,4,16,512]{3,2,1,0:T(8,128)}, u32[]{:S(2)}, u32[]{:S(2)}) collective-permute-start(f32[6,4,16,512]{3,2,1,0:T(8,128)S(1)} %get-tuple-element.357), channel_id=1, source_target_pairs={{0,1},{1,2},{2,3},{3,4},{4,5},{5,6},{6,7},{7,8},{8,9},{9,10},{10,1... | collective-permute-start | bytes 2359304 | tf_op jit(solution)/shard_map/while/body/eval_jaxpr/ppermute | solution.py:21
  178.5 15.0 %collective-permute-done.2 = f32[6,4,16,512]{3,2,1,0:T(8,128)} collective-permute-done((f32[6,4,16,512]{3,2,1,0:T(8,128)}, f32[6,4,16,512]{3,2,1,0:T(8,128)}, u32[]{:S(2)}, u32[]{:S(2)}) %collective-permute-start.2) | collective-permute-done | bytes 786464 | tf_op jit(solution)/shard_map/while/body/eval_jaxpr/ppermute | solution.py:24
  193.5 15.5 %collective-permute-done.3 = f32[6,4,16,512]{3,2,1,0:T(8,128)} collective-permute-done((f32[6,4,16,512]{3,2,1,0:T(8,128)S(1)}, f32[6,4,16,512]{3,2,1,0:T(8,128)}, u32[]{:S(2)}, u32[]{:S(2)}) %collective-permute-start.3) | collective-permute-done | bytes 786464 | tf_op jit(solution)/shard_map/while/body/eval_jaxpr/ppermute | solution.py:21
  209.0 1.8 pad_maximum_fusion.25
  211.8 0.7 add_multiply_fusion.15
  214.1 0.7 add_multiply_fusion.17
  216.5 0.7 add_multiply_fusion.19
  221.2 1.3 collective-permute-start
  222.5 3.1 collective-permute-start.1
  227.2 1.1 fusion.57
  228.3 1.3 collective-permute-start.2
  229.6 6.0 %collective-permute-start.3 = (f32[6,4,16,512]{3,2,1,0:T(8,128)S(1)}, f32[6,4,16,512]{3,2,1,0:T(8,128)}, u32[]{:S(2)}, u32[]{:S(2)}) collective-permute-start(f32[6,4,16,512]{3,2,1,0:T(8,128)S(1)} %get-tuple-element.357), channel_id=1, source_target_pairs={{0,1},{1,2},{2,3},{3,4},{4,5},{5,6},{6,7},{7,8},{8,9},{9,10},{10,1... | collective-permute-start | bytes 2359304 | tf_op jit(solution)/shard_map/while/body/eval_jaxpr/ppermute | solution.py:21
  236.5 15.0 %collective-permute-done.2 = f32[6,4,16,512]{3,2,1,0:T(8,128)} collective-permute-done((f32[6,4,16,512]{3,2,1,0:T(8,128)}, f32[6,4,16,512]{3,2,1,0:T(8,128)}, u32[]{:S(2)}, u32[]{:S(2)}) %collective-permute-start.2) | collective-permute-done | bytes 786464 | tf_op jit(solution)/shard_map/while/body/eval_jaxpr/ppermute | solution.py:24
  251.5 17.1 %collective-permute-done.3 = f32[6,4,16,512]{3,2,1,0:T(8,128)} collective-permute-done((f32[6,4,16,512]{3,2,1,0:T(8,128)S(1)}, f32[6,4,16,512]{3,2,1,0:T(8,128)}, u32[]{:S(2)}, u32[]{:S(2)}) %collective-permute-start.3) | collective-permute-done | bytes 786464 | tf_op jit(solution)/shard_map/while/body/eval_jaxpr/ppermute | solution.py:21
  268.6 1.8 pad_maximum_fusion.25
  271.5 0.7 add_multiply_fusion.15
  273.8 0.7 add_multiply_fusion.17
  276.1 0.7 add_multiply_fusion.19
  281.9 18.3 %all-reduce.52.cloned.1.call-done = f32[2,2,2,6,512]{4,3,1,0,2:T(8,128)} async-done(((f32[2,2,2,6,512]{4,3,1,0,2:T(8,128)}), f32[2,2,2,6,512]{4,3,1,0,2:T(8,128)}) %all-reduce.52.cloned.1.call-update) | async-done | bytes 98320 | tf_op jit(solution)/shard_map/psum | solution.py:31
  300.2 1.9 fusion.13
  302.1 1.9 convolution_add_fusion.1
  307.4 1.5 copy.52
  310.2 110.9 %all-reduce.54.cloned.1.call-done = f32[96,2,2,2,256]{4,3,2,1,0:T(2,128)} async-done(((f32[96,2,2,2,256]{4,3,2,1,0:T(2,128)}), f32[96,2,2,2,256]{4,3,2,1,0:T(2,128)}) %all-reduce.54.cloned.1.call-update) | async-done | bytes 786448
  421.0 0.8 constant_dynamic-slice_fusion
  (335 shorter events, 40.8 us)
Async XLA Ops:
  7.2 293.0 %all-reduce.52.cloned.1.call-start = ((), (), s32[]{:S(2)}) async-start(), calls=%async_computation | async-start | bytes 262144 | tf_op jit(solution)/shard_map/psum | solution.py:31
  17.0 3.8 collective-permute-start.4
  19.4 3.3 collective-permute-start.5
  22.9 21.3 %collective-permute-start.6 = (f32[3,4,16,512]{3,2,1,0:T(8,128)S(1)}, f32[3,4,16,512]{3,2,1,0:T(8,128)S(1)}, u32[]{:S(2)}, u32[]{:S(2)}) collective-permute-start(f32[3,4,16,512]{3,2,1,0:T(8,128)S(1)} %get-tuple-element.239), channel_id=1, source_target_pairs={{0,1},{1,2},{2,3},{3,4},{4,5},{5,6},{6,7},{7,8},{8,9},{9,10},{10,1... | collective-permute-start | bytes 1179656 | tf_op jit(solution)/shard_map/ppermute | solution.py:21
  27.1 19.0 %collective-permute-start.7 = (f32[3,4,16,512]{3,2,1,0:T(8,128)S(1)}, f32[3,4,16,512]{3,2,1,0:T(8,128)S(1)}, u32[]{:S(2)}, u32[]{:S(2)}) collective-permute-start(f32[3,4,16,512]{3,2,1,0:T(8,128)S(1)} %get-tuple-element.240), channel_id=1, source_target_pairs={{1,0},{2,1},{3,2},{4,3},{5,4},{6,5},{7,6},{8,7},{9,8},{10,9},{11,1... | collective-permute-start | bytes 1179656 | tf_op jit(solution)/shard_map/ppermute | solution.py:24
  34.1 12.4 %copy-start.1 = (f32[6,6,8,512]{3,2,1,0:T(8,128)S(1)}, f32[6,6,8,512]{3,2,1,0:T(8,128)}, u32[]{:S(2)}) copy-start(f32[6,6,8,512]{3,2,1,0:T(8,128)} %param.7) | copy-start | bytes 1769476
  46.6 235.2 %copy-start.7 = (s32[6]{0:T(128)S(1)}, s32[6]{0:T(128)}, u32[]{:S(2)}) copy-start(s32[6]{0:T(128)} %iota_add_fusion.1) | copy-start | bytes 76
  46.9 5.8 %collective-permute-start = (f32[6,6,4,512]{3,2,1,0:T(4,128)S(1)}, f32[6,6,4,512]{3,2,1,0:T(4,128)S(1)}, u32[]{:S(2)}, u32[]{:S(2)}) collective-permute-start(f32[6,6,4,512]{3,2,1,0:T(4,128)S(1)} %get-tuple-element.354), channel_id=1, source_target_pairs={{16,0},{17,1},{18,2},{19,3},{20,4},{21,5},{22,6},{23,7},{24,8},{25... | collective-permute-start | bytes 884744 | tf_op jit(solution)/shard_map/while/body/eval_jaxpr/ppermute | solution.py:24
  48.2 4.5 %collective-permute-start.1 = (f32[6,6,4,512]{3,2,1,0:T(4,128)S(1)}, f32[6,6,4,512]{3,2,1,0:T(4,128)S(1)}, u32[]{:S(2)}, u32[]{:S(2)}) collective-permute-start(f32[6,6,4,512]{3,2,1,0:T(4,128)S(1)} %get-tuple-element.355), channel_id=1, source_target_pairs={{0,16},{1,17},{2,18},{3,19},{4,20},{5,21},{6,22},{7,23},{8,24},{9,... | collective-permute-start | bytes 884744 | tf_op jit(solution)/shard_map/while/body/eval_jaxpr/ppermute | solution.py:21
  54.0 22.6 %collective-permute-start.2 = (f32[6,4,16,512]{3,2,1,0:T(8,128)}, f32[6,4,16,512]{3,2,1,0:T(8,128)}, u32[]{:S(2)}, u32[]{:S(2)}) collective-permute-start(f32[6,4,16,512]{3,2,1,0:T(8,128)} %get-tuple-element.356), channel_id=1, source_target_pairs={{1,0},{2,1},{3,2},{4,3},{5,4},{6,5},{7,6},{8,7},{9,8},{10,9},{11,1... | collective-permute-start | bytes 2359304 | tf_op jit(solution)/shard_map/while/body/eval_jaxpr/ppermute | solution.py:24
  55.3 36.0 %collective-permute-start.3 = (f32[6,4,16,512]{3,2,1,0:T(8,128)S(1)}, f32[6,4,16,512]{3,2,1,0:T(8,128)}, u32[]{:S(2)}, u32[]{:S(2)}) collective-permute-start(f32[6,4,16,512]{3,2,1,0:T(8,128)S(1)} %get-tuple-element.357), channel_id=1, source_target_pairs={{0,1},{1,2},{2,3},{3,4},{4,5},{5,6},{6,7},{7,8},{8,9},{9,10},{10,1... | collective-permute-start | bytes 2359304 | tf_op jit(solution)/shard_map/while/body/eval_jaxpr/ppermute | solution.py:21
  103.5 5.8 %collective-permute-start = (f32[6,6,4,512]{3,2,1,0:T(4,128)S(1)}, f32[6,6,4,512]{3,2,1,0:T(4,128)S(1)}, u32[]{:S(2)}, u32[]{:S(2)}) collective-permute-start(f32[6,6,4,512]{3,2,1,0:T(4,128)S(1)} %get-tuple-element.354), channel_id=1, source_target_pairs={{16,0},{17,1},{18,2},{19,3},{20,4},{21,5},{22,6},{23,7},{24,8},{25... | collective-permute-start | bytes 884744 | tf_op jit(solution)/shard_map/while/body/eval_jaxpr/ppermute | solution.py:24
  104.8 4.5 %collective-permute-start.1 = (f32[6,6,4,512]{3,2,1,0:T(4,128)S(1)}, f32[6,6,4,512]{3,2,1,0:T(4,128)S(1)}, u32[]{:S(2)}, u32[]{:S(2)}) collective-permute-start(f32[6,6,4,512]{3,2,1,0:T(4,128)S(1)} %get-tuple-element.355), channel_id=1, source_target_pairs={{0,16},{1,17},{2,18},{3,19},{4,20},{5,21},{6,22},{7,23},{8,24},{9,... | collective-permute-start | bytes 884744 | tf_op jit(solution)/shard_map/while/body/eval_jaxpr/ppermute | solution.py:21
  110.6 23.2 %collective-permute-start.2 = (f32[6,4,16,512]{3,2,1,0:T(8,128)}, f32[6,4,16,512]{3,2,1,0:T(8,128)}, u32[]{:S(2)}, u32[]{:S(2)}) collective-permute-start(f32[6,4,16,512]{3,2,1,0:T(8,128)} %get-tuple-element.356), channel_id=1, source_target_pairs={{1,0},{2,1},{3,2},{4,3},{5,4},{6,5},{7,6},{8,7},{9,8},{10,9},{11,1... | collective-permute-start | bytes 2359304 | tf_op jit(solution)/shard_map/while/body/eval_jaxpr/ppermute | solution.py:24
  111.9 39.0 %collective-permute-start.3 = (f32[6,4,16,512]{3,2,1,0:T(8,128)S(1)}, f32[6,4,16,512]{3,2,1,0:T(8,128)}, u32[]{:S(2)}, u32[]{:S(2)}) collective-permute-start(f32[6,4,16,512]{3,2,1,0:T(8,128)S(1)} %get-tuple-element.357), channel_id=1, source_target_pairs={{0,1},{1,2},{2,3},{3,4},{4,5},{5,6},{6,7},{7,8},{8,9},{9,10},{10,1... | collective-permute-start | bytes 2359304 | tf_op jit(solution)/shard_map/while/body/eval_jaxpr/ppermute | solution.py:21
  163.2 5.8 %collective-permute-start = (f32[6,6,4,512]{3,2,1,0:T(4,128)S(1)}, f32[6,6,4,512]{3,2,1,0:T(4,128)S(1)}, u32[]{:S(2)}, u32[]{:S(2)}) collective-permute-start(f32[6,6,4,512]{3,2,1,0:T(4,128)S(1)} %get-tuple-element.354), channel_id=1, source_target_pairs={{16,0},{17,1},{18,2},{19,3},{20,4},{21,5},{22,6},{23,7},{24,8},{25... | collective-permute-start | bytes 884744 | tf_op jit(solution)/shard_map/while/body/eval_jaxpr/ppermute | solution.py:24
  164.5 4.5 %collective-permute-start.1 = (f32[6,6,4,512]{3,2,1,0:T(4,128)S(1)}, f32[6,6,4,512]{3,2,1,0:T(4,128)S(1)}, u32[]{:S(2)}, u32[]{:S(2)}) collective-permute-start(f32[6,6,4,512]{3,2,1,0:T(4,128)S(1)} %get-tuple-element.355), channel_id=1, source_target_pairs={{0,16},{1,17},{2,18},{3,19},{4,20},{5,21},{6,22},{7,23},{8,24},{9,... | collective-permute-start | bytes 884744 | tf_op jit(solution)/shard_map/while/body/eval_jaxpr/ppermute | solution.py:21
  170.3 23.2 %collective-permute-start.2 = (f32[6,4,16,512]{3,2,1,0:T(8,128)}, f32[6,4,16,512]{3,2,1,0:T(8,128)}, u32[]{:S(2)}, u32[]{:S(2)}) collective-permute-start(f32[6,4,16,512]{3,2,1,0:T(8,128)} %get-tuple-element.356), channel_id=1, source_target_pairs={{1,0},{2,1},{3,2},{4,3},{5,4},{6,5},{7,6},{8,7},{9,8},{10,9},{11,1... | collective-permute-start | bytes 2359304 | tf_op jit(solution)/shard_map/while/body/eval_jaxpr/ppermute | solution.py:24
  171.6 37.4 %collective-permute-start.3 = (f32[6,4,16,512]{3,2,1,0:T(8,128)S(1)}, f32[6,4,16,512]{3,2,1,0:T(8,128)}, u32[]{:S(2)}, u32[]{:S(2)}) collective-permute-start(f32[6,4,16,512]{3,2,1,0:T(8,128)S(1)} %get-tuple-element.357), channel_id=1, source_target_pairs={{0,1},{1,2},{2,3},{3,4},{4,5},{5,6},{6,7},{7,8},{8,9},{9,10},{10,1... | collective-permute-start | bytes 2359304 | tf_op jit(solution)/shard_map/while/body/eval_jaxpr/ppermute | solution.py:21
  221.2 5.8 %collective-permute-start = (f32[6,6,4,512]{3,2,1,0:T(4,128)S(1)}, f32[6,6,4,512]{3,2,1,0:T(4,128)S(1)}, u32[]{:S(2)}, u32[]{:S(2)}) collective-permute-start(f32[6,6,4,512]{3,2,1,0:T(4,128)S(1)} %get-tuple-element.354), channel_id=1, source_target_pairs={{16,0},{17,1},{18,2},{19,3},{20,4},{21,5},{22,6},{23,7},{24,8},{25... | collective-permute-start | bytes 884744 | tf_op jit(solution)/shard_map/while/body/eval_jaxpr/ppermute | solution.py:24
  222.5 4.5 %collective-permute-start.1 = (f32[6,6,4,512]{3,2,1,0:T(4,128)S(1)}, f32[6,6,4,512]{3,2,1,0:T(4,128)S(1)}, u32[]{:S(2)}, u32[]{:S(2)}) collective-permute-start(f32[6,6,4,512]{3,2,1,0:T(4,128)S(1)} %get-tuple-element.355), channel_id=1, source_target_pairs={{0,16},{1,17},{2,18},{3,19},{4,20},{5,21},{6,22},{7,23},{8,24},{9,... | collective-permute-start | bytes 884744 | tf_op jit(solution)/shard_map/while/body/eval_jaxpr/ppermute | solution.py:21
  228.3 23.2 %collective-permute-start.2 = (f32[6,4,16,512]{3,2,1,0:T(8,128)}, f32[6,4,16,512]{3,2,1,0:T(8,128)}, u32[]{:S(2)}, u32[]{:S(2)}) collective-permute-start(f32[6,4,16,512]{3,2,1,0:T(8,128)} %get-tuple-element.356), channel_id=1, source_target_pairs={{1,0},{2,1},{3,2},{4,3},{5,4},{6,5},{7,6},{8,7},{9,8},{10,9},{11,1... | collective-permute-start | bytes 2359304 | tf_op jit(solution)/shard_map/while/body/eval_jaxpr/ppermute | solution.py:24
  229.6 39.0 %collective-permute-start.3 = (f32[6,4,16,512]{3,2,1,0:T(8,128)S(1)}, f32[6,4,16,512]{3,2,1,0:T(8,128)}, u32[]{:S(2)}, u32[]{:S(2)}) collective-permute-start(f32[6,4,16,512]{3,2,1,0:T(8,128)S(1)} %get-tuple-element.357), channel_id=1, source_target_pairs={{0,1},{1,2},{2,3},{3,4},{4,5},{5,6},{6,7},{7,8},{8,9},{9,10},{10,1... | collective-permute-start | bytes 2359304 | tf_op jit(solution)/shard_map/while/body/eval_jaxpr/ppermute | solution.py:21
  280.7 25.1 %copy-start = (f32[6,6,8,512]{3,2,1,0:T(8,128)}, f32[6,6,8,512]{3,2,1,0:T(8,128)S(1)}, u32[]{:S(2)}) copy-start(f32[6,6,8,512]{3,2,1,0:T(8,128)S(1)} %get-tuple-element.168) | copy-start | bytes 1769476
  280.7 23.7 %copy-start.4 = (f32[1,512,256]{2,1,0:T(8,128)S(1)}, f32[1,512,256]{2,1,0:T(8,128)}, u32[]{:S(2)}) copy-start(f32[1,512,256]{2,1,0:T(8,128)} %get-tuple-element.243) | copy-start | bytes 1572868
  280.7 23.7 %copy-start.5 = (f32[1,512,256]{2,1,0:T(8,128)S(1)}, f32[1,512,256]{2,1,0:T(8,128)}, u32[]{:S(2)}) copy-start(f32[1,512,256]{2,1,0:T(8,128)} %get-tuple-element.244) | copy-start | bytes 1572868
  280.8 24.4 %copy-start.2 = (f32[1,512,256]{2,1,0:T(8,128)S(1)}, f32[1,512,256]{2,1,0:T(8,128)}, u32[]{:S(2)}) copy-start(f32[1,512,256]{2,1,0:T(8,128)} %get-tuple-element.245) | copy-start | bytes 1572868
  280.8 24.4 %copy-start.3 = (f32[1,512,256]{2,1,0:T(8,128)S(1)}, f32[1,512,256]{2,1,0:T(8,128)}, u32[]{:S(2)}) copy-start(f32[1,512,256]{2,1,0:T(8,128)} %get-tuple-element.246) | copy-start | bytes 1572868
  281.5 139.6 %all-reduce.54.cloned.1.call-start = ((), (), s32[]{:S(2)}) async-start(), calls=%async_computation.1 | async-start | bytes 1572864
  300.2 4.3 %copy-start.6 = (f32[2,2,2,6,512]{4,3,1,0,2:T(8,128)S(1)}, f32[2,2,2,6,512]{4,3,1,0,2:T(8,128)}, u32[]{:S(2)}) copy-start(f32[2,2,2,6,512]{4,3,1,0,2:T(8,128)} %all-reduce.52.cloned.1.call-done) | copy-start | bytes 294916
  306.3 2.6 copy-start.8
Sparse Core Ops, SparseCore 0:
  281.6 18.5 all-reduce.51
  309.0 111.9 all-reduce.53
where the time goes:
time: 430 us; the launch traced here: 429 us
  waiting for transfers between devices  267 us (62%)
  starting transfers between devices  55.6 us (13%)
  other arithmetic  52 us (12%)
  local copies, waits for them, and re-layouts  22.5 us (5%)
  between operations  15 us (3%)
  loops' own time  9.67 us (2%)
  matrix products  7.03 us (2%)
    unnamed x3, waiting for transfers between devices  111 us
    ppermute x10, waiting for transfers between devices, padded_2(): lax.ppermute(lax.slice_in_dim(block, block.shape[dim] - width, None, axis...  74.6 us
    ppermute x10, waiting for transfers between devices, padded_2(): lax.ppermute(lax.slice_in_dim(block, 0, width, axis=dim), axis, backward)  63.6 us
    ppermute x10, starting transfers between devices, padded_2(): lax.ppermute(lax.slice_in_dim(block, block.shape[dim] - width, None, axis...  42.4 us
    psum x1, waiting for transfers between devices, from_root(): return lax.psum(block, axis)  18.3 us
    ppermute x10, starting transfers between devices, padded_2(): lax.ppermute(lax.slice_in_dim(block, 0, width, axis=dim), axis, backward)  12.9 us
    another operation x1, loops' own time, local(): lax.fori_loop(0, STEPS // HALO_STEPS, one_block, (fields, empty_spectrum))  9.67 us
    mul x12, other arithmetic, yee_step(): (elec_y + factor * (backward_diff(magn_x, 1) - backward_diff(magn_z, 0)))...  8.82 us
  transfers between devices with their start and end apart: 22, of which 13 were waited for; matrix products, arithmetic and copies ran while one was open for 2% of the time, Pallas kernels for 0%

commit v1 on v0

--- a/solution.py
+++ b/solution.py
@@ -28,7 +28,7 @@
 
 def from_root(block, axis, owner):
     block = jnp.where(lax.axis_index(axis) == owner, block, jnp.zeros_like(block))
-    return lax.psum(block, axis)
+    return jnp.sum(lax.all_gather(block, axis), axis=0)
 
 
 def forward_diff(field, along):

time: 430 us -> 413 us (0.960)
  waiting for transfers between devices: 267 us -> 248 us
    psum x1 -> x0, waiting for transfers between devices: 18.3 us -> none  [from_root(): return lax.psum(block, axis)]
    unnamed x3 -> x2, waiting for transfers between devices: 111 us -> 110 us
  transfers between devices with their start and end apart: 22 -> 21, of which waited for: 13 -> 12; matrix products, arithmetic and copies ran while one was open for 2% -> 2% of each run, Pallas kernels for 0% -> 0%
where the time goes in v1:
time: 413 us; the launch traced here: 412 us
  waiting for transfers between devices  248 us (60%)
  starting transfers between devices  55.4 us (13%)
  other arithmetic  51.6 us (12%)
  local copies, waits for them, and re-layouts  22.6 us (5%)
  between operations  15.1 us (4%)
  loops' own time  9.68 us (2%)
  matrix products  6.96 us (2%)
    unnamed x2, waiting for transfers between devices  110 us
    ppermute x10, waiting for transfers between devices, padded_2(): lax.ppermute(lax.slice_in_dim(block, block.shape[dim] - width, None, axis...  75.1 us
    ppermute x10, waiting for transfers between devices, padded_2(): lax.ppermute(lax.slice_in_dim(block, 0, width, axis=dim), axis, backward)  63 us
    ppermute x10, starting transfers between devices, padded_2(): lax.ppermute(lax.slice_in_dim(block, block.shape[dim] - width, None, axis...  42.4 us
    ppermute x10, starting transfers between devices, padded_2(): lax.ppermute(lax.slice_in_dim(block, 0, width, axis=dim), axis, backward)  12.9 us
    another operation x1, loops' own time, local(): lax.fori_loop(0, STEPS // HALO_STEPS, one_block, (fields, empty_spectrum))  9.68 us
    mul x12, other arithmetic, yee_step(): (elec_y + factor * (backward_diff(magn_x, 1) - backward_diff(magn_z, 0)))...  8.82 us
    slice x92, local copies, waits for them, and re-layouts, forward_diff(): ahead = lax.slice_in_dim(field, 1, length, axis=along)  8.37 us
  transfers between devices with their start and end apart: 21, of which 12 were waited for; matrix products, arithmetic and copies ran while one was open for 2% of the time, Pallas kernels for 0%

profile of v1, /device:TPU:0, one launch (start us, length us, event | category | flops | bytes accessed | tf_op | source)
XLA Modules:
  0.0 412.0 jit_solution(7857703062916455113)
XLA Ops:
  7.2 1.5 fusion.48
  8.7 1.5 fusion.47
  10.1 0.9 convert_bitcast_fusion.1
  11.0 3.4 select_bitcast_fusion.1
  14.5 2.5 select_bitcast_fusion
  17.0 2.4 collective-permute-start.4
  19.4 1.3 collective-permute-start.5
  20.8 0.7 sine_multiply_fusion.3
  21.5 1.2 collective-permute-done.5
  22.9 4.2 %collective-permute-start.6 = (f32[3,4,16,512]{3,2,1,0:T(8,128)S(1)}, f32[3,4,16,512]{3,2,1,0:T(8,128)S(1)}, u32[]{:S(2)}, u32[]{:S(2)}) collective-permute-start(f32[3,4,16,512]{3,2,1,0:T(8,128)S(1)} %get-tuple-element.239), channel_id=1, source_target_pairs={{0,1},{1,2},{2,3},{3,4},{4,5},{5,6},{6,7},{7,8},{8,9},{9,10},{10,1... | collective-permute-start | bytes 1179656 | tf_op jit(solution)/shard_map/ppermute | solution.py:21
  27.1 1.3 collective-permute-start.7
  28.5 5.1 %cosine_multiply_fusion.1 = (f32[1,512,256]{2,1,0:T(8,128)}, f32[1,512,256]{2,1,0:T(8,128)}, f32[1,512,256]{2,1,0:T(8,128)}, f32[1,512,256]{2,1,0:T(8,128)}) fusion(s32[256]{0:T(256)S(1)} %iota_add_fusion), kind=kLoop, calls=%fused_computation.100 | loop fusion | flops 4456448 | bytes 2098176 | tf_op jit(solution)/shard_map/div | solution.py:97
  33.6 10.6 %collective-permute-done.6 = f32[3,4,16,512]{3,2,1,0:T(8,128)S(1)} collective-permute-done((f32[3,4,16,512]{3,2,1,0:T(8,128)S(1)}, f32[3,4,16,512]{3,2,1,0:T(8,128)S(1)}, u32[]{:S(2)}, u32[]{:S(2)}) %collective-permute-start.6) | collective-permute-done | bytes 393248 | tf_op jit(solution)/shard_map/ppermute | solution.py:21
  44.2 1.9 collective-permute-done.7
  46.6 234.1 %while.16 = (s32[]{:T(128)}, f32[6,6,8,512]{3,2,1,0:T(8,128)S(1)}, f32[2,2,2,6,512]{4,3,2,1,0:T(8,128)S(1)}, f32[14,16,512]{2,1,0:T(8,128)S(1)}, f32[14,16,512]{...) while((s32[]{:T(128)}, f32[6,6,8,512]{3,2,1,0:T(8,128)S(1)}, ...), condition=%wide.region_1.2_spmd.clone, body=%wide.region_0.1_spmd.clone.sunk | while | flops 24691188 | bytes 132281024 | solution.py:162
  46.9 1.3 collective-permute-start
  48.2 3.1 collective-permute-start.1
  52.9 1.1 fusion.58
  54.0 1.3 collective-permute-start.2
  55.3 5.5 %collective-permute-start.3 = (f32[6,4,16,512]{3,2,1,0:T(8,128)S(1)}, f32[6,4,16,512]{3,2,1,0:T(8,128)}, u32[]{:S(2)}, u32[]{:S(2)}) collective-permute-start(f32[6,4,16,512]{3,2,1,0:T(8,128)S(1)} %get-tuple-element.359), channel_id=1, source_target_pairs={{0,1},{1,2},{2,3},{3,4},{4,5},{5,6},{6,7},{7,8},{8,9},{9,10},{10,1... | collective-permute-start | bytes 2359304 | tf_op jit(solution)/shard_map/while/body/eval_jaxpr/ppermute | solution.py:21
  61.6 15.0 %collective-permute-done.2 = f32[6,4,16,512]{3,2,1,0:T(8,128)} collective-permute-done((f32[6,4,16,512]{3,2,1,0:T(8,128)}, f32[6,4,16,512]{3,2,1,0:T(8,128)}, u32[]{:S(2)}, u32[]{:S(2)}) %collective-permute-start.2) | collective-permute-done | bytes 786464 | tf_op jit(solution)/shard_map/while/body/eval_jaxpr/ppermute | solution.py:24
  76.6 14.7 %collective-permute-done.3 = f32[6,4,16,512]{3,2,1,0:T(8,128)} collective-permute-done((f32[6,4,16,512]{3,2,1,0:T(8,128)S(1)}, f32[6,4,16,512]{3,2,1,0:T(8,128)}, u32[]{:S(2)}, u32[]{:S(2)}) %collective-permute-start.3) | collective-permute-done | bytes 786464 | tf_op jit(solution)/shard_map/while/body/eval_jaxpr/ppermute | solution.py:21
  91.3 1.8 pad_maximum_fusion.25
  94.2 0.7 add_multiply_fusion.15
  96.5 0.7 add_multiply_fusion.17
  98.8 0.7 add_multiply_fusion.19
  103.5 1.3 collective-permute-start
  104.8 3.1 collective-permute-start.1
  109.5 1.1 fusion.58
  110.6 1.3 collective-permute-start.2
  111.9 6.0 %collective-permute-start.3 = (f32[6,4,16,512]{3,2,1,0:T(8,128)S(1)}, f32[6,4,16,512]{3,2,1,0:T(8,128)}, u32[]{:S(2)}, u32[]{:S(2)}) collective-permute-start(f32[6,4,16,512]{3,2,1,0:T(8,128)S(1)} %get-tuple-element.359), channel_id=1, source_target_pairs={{0,1},{1,2},{2,3},{3,4},{4,5},{5,6},{6,7},{7,8},{8,9},{9,10},{10,1... | collective-permute-start | bytes 2359304 | tf_op jit(solution)/shard_map/while/body/eval_jaxpr/ppermute | solution.py:21
  118.9 15.0 %collective-permute-done.2 = f32[6,4,16,512]{3,2,1,0:T(8,128)} collective-permute-done((f32[6,4,16,512]{3,2,1,0:T(8,128)}, f32[6,4,16,512]{3,2,1,0:T(8,128)}, u32[]{:S(2)}, u32[]{:S(2)}) %collective-permute-start.2) | collective-permute-done | bytes 786464 | tf_op jit(solution)/shard_map/while/body/eval_jaxpr/ppermute | solution.py:24
  133.8 17.1 %collective-permute-done.3 = f32[6,4,16,512]{3,2,1,0:T(8,128)} collective-permute-done((f32[6,4,16,512]{3,2,1,0:T(8,128)S(1)}, f32[6,4,16,512]{3,2,1,0:T(8,128)}, u32[]{:S(2)}, u32[]{:S(2)}) %collective-permute-start.3) | collective-permute-done | bytes 786464 | tf_op jit(solution)/shard_map/while/body/eval_jaxpr/ppermute | solution.py:21
  151.0 1.8 pad_maximum_fusion.25
  153.8 0.7 add_multiply_fusion.15
  158.5 0.7 add_multiply_fusion.19
  163.2 1.3 collective-permute-start
  164.5 3.1 collective-permute-start.1
  169.2 1.1 fusion.58
  170.3 1.3 collective-permute-start.2
  171.6 6.0 %collective-permute-start.3 = (f32[6,4,16,512]{3,2,1,0:T(8,128)S(1)}, f32[6,4,16,512]{3,2,1,0:T(8,128)}, u32[]{:S(2)}, u32[]{:S(2)}) collective-permute-start(f32[6,4,16,512]{3,2,1,0:T(8,128)S(1)} %get-tuple-element.359), channel_id=1, source_target_pairs={{0,1},{1,2},{2,3},{3,4},{4,5},{5,6},{6,7},{7,8},{8,9},{9,10},{10,1... | collective-permute-start | bytes 2359304 | tf_op jit(solution)/shard_map/while/body/eval_jaxpr/ppermute | solution.py:21
  178.5 15.0 %collective-permute-done.2 = f32[6,4,16,512]{3,2,1,0:T(8,128)} collective-permute-done((f32[6,4,16,512]{3,2,1,0:T(8,128)}, f32[6,4,16,512]{3,2,1,0:T(8,128)}, u32[]{:S(2)}, u32[]{:S(2)}) %collective-permute-start.2) | collective-permute-done | bytes 786464 | tf_op jit(solution)/shard_map/while/body/eval_jaxpr/ppermute | solution.py:24
  193.5 15.5 %collective-permute-done.3 = f32[6,4,16,512]{3,2,1,0:T(8,128)} collective-permute-done((f32[6,4,16,512]{3,2,1,0:T(8,128)S(1)}, f32[6,4,16,512]{3,2,1,0:T(8,128)}, u32[]{:S(2)}, u32[]{:S(2)}) %collective-permute-start.3) | collective-permute-done | bytes 786464 | tf_op jit(solution)/shard_map/while/body/eval_jaxpr/ppermute | solution.py:21
  209.0 1.8 pad_maximum_fusion.25
  211.8 0.7 add_multiply_fusion.15
  214.1 0.7 add_multiply_fusion.17
  216.5 0.7 add_multiply_fusion.19
  221.2 1.3 collective-permute-start
  222.5 3.1 collective-permute-start.1
  227.2 1.1 fusion.58
  228.3 1.3 collective-permute-start.2
  229.6 6.0 %collective-permute-start.3 = (f32[6,4,16,512]{3,2,1,0:T(8,128)S(1)}, f32[6,4,16,512]{3,2,1,0:T(8,128)}, u32[]{:S(2)}, u32[]{:S(2)}) collective-permute-start(f32[6,4,16,512]{3,2,1,0:T(8,128)S(1)} %get-tuple-element.359), channel_id=1, source_target_pairs={{0,1},{1,2},{2,3},{3,4},{4,5},{5,6},{6,7},{7,8},{8,9},{9,10},{10,1... | collective-permute-start | bytes 2359304 | tf_op jit(solution)/shard_map/while/body/eval_jaxpr/ppermute | solution.py:21
  236.5 15.0 %collective-permute-done.2 = f32[6,4,16,512]{3,2,1,0:T(8,128)} collective-permute-done((f32[6,4,16,512]{3,2,1,0:T(8,128)}, f32[6,4,16,512]{3,2,1,0:T(8,128)}, u32[]{:S(2)}, u32[]{:S(2)}) %collective-permute-start.2) | collective-permute-done | bytes 786464 | tf_op jit(solution)/shard_map/while/body/eval_jaxpr/ppermute | solution.py:24
  251.5 17.1 %collective-permute-done.3 = f32[6,4,16,512]{3,2,1,0:T(8,128)} collective-permute-done((f32[6,4,16,512]{3,2,1,0:T(8,128)S(1)}, f32[6,4,16,512]{3,2,1,0:T(8,128)}, u32[]{:S(2)}, u32[]{:S(2)}) %collective-permute-start.3) | collective-permute-done | bytes 786464 | tf_op jit(solution)/shard_map/while/body/eval_jaxpr/ppermute | solution.py:21
  268.6 1.8 pad_maximum_fusion.25
  271.5 0.7 add_multiply_fusion.15
  273.8 0.7 add_multiply_fusion.17
  276.1 0.7 add_multiply_fusion.19
  280.9 2.3 all-gather
  283.4 1.8 fusion.14
  285.3 1.8 fusion.13
  290.6 1.5 copy.52
  293.4 110.3 %all-reduce.51.cloned.1.call-done = f32[96,2,2,2,256]{4,3,2,1,0:T(2,128)} async-done(((f32[96,2,2,2,256]{4,3,2,1,0:T(2,128)}), f32[96,2,2,2,256]{4,3,2,1,0:T(2,128)}) %all-reduce.51.cloned.1.call-update) | async-done | bytes 786448
  403.7 0.8 constant_dynamic-slice_fusion
  (339 shorter events, 40.2 us)
Async XLA Ops:
  7.2 396.6 %all-reduce.51.cloned.1.call-start = ((), (), s32[]{:S(2)}) async-start(), calls=%async_computation | async-start | bytes 1572864
  17.0 4.5 %collective-permute-start.4 = (f32[3,6,4,512]{3,2,1,0:T(4,128)S(1)}, f32[3,6,4,512]{3,2,1,0:T(4,128)S(1)}, u32[]{:S(2)}, u32[]{:S(2)}) collective-permute-start(f32[3,6,4,512]{3,2,1,0:T(4,128)S(1)} %get-tuple-element.241), channel_id=1, source_target_pairs={{0,16},{1,17},{2,18},{3,19},{4,20},{5,21},{6,22},{7,23},{8,24},{9,... | collective-permute-start | bytes 442376 | tf_op jit(solution)/shard_map/ppermute | solution.py:21
  19.4 3.3 collective-permute-start.5
  22.9 21.3 %collective-permute-start.6 = (f32[3,4,16,512]{3,2,1,0:T(8,128)S(1)}, f32[3,4,16,512]{3,2,1,0:T(8,128)S(1)}, u32[]{:S(2)}, u32[]{:S(2)}) collective-permute-start(f32[3,4,16,512]{3,2,1,0:T(8,128)S(1)} %get-tuple-element.239), channel_id=1, source_target_pairs={{0,1},{1,2},{2,3},{3,4},{4,5},{5,6},{6,7},{7,8},{8,9},{9,10},{10,1... | collective-permute-start | bytes 1179656 | tf_op jit(solution)/shard_map/ppermute | solution.py:21
  27.1 19.0 %collective-permute-start.7 = (f32[3,4,16,512]{3,2,1,0:T(8,128)S(1)}, f32[3,4,16,512]{3,2,1,0:T(8,128)S(1)}, u32[]{:S(2)}, u32[]{:S(2)}) collective-permute-start(f32[3,4,16,512]{3,2,1,0:T(8,128)S(1)} %get-tuple-element.240), channel_id=1, source_target_pairs={{1,0},{2,1},{3,2},{4,3},{5,4},{6,5},{7,6},{8,7},{9,8},{10,9},{11,1... | collective-permute-start | bytes 1179656 | tf_op jit(solution)/shard_map/ppermute | solution.py:24
  33.6 12.9 %copy-start.1 = (f32[6,6,8,512]{3,2,1,0:T(8,128)S(1)}, f32[6,6,8,512]{3,2,1,0:T(8,128)}, u32[]{:S(2)}) copy-start(f32[6,6,8,512]{3,2,1,0:T(8,128)} %param.7) | copy-start | bytes 1769476
  46.9 5.8 %collective-permute-start = (f32[6,6,4,512]{3,2,1,0:T(4,128)S(1)}, f32[6,6,4,512]{3,2,1,0:T(4,128)S(1)}, u32[]{:S(2)}, u32[]{:S(2)}) collective-permute-start(f32[6,6,4,512]{3,2,1,0:T(4,128)S(1)} %get-tuple-element.356), channel_id=1, source_target_pairs={{16,0},{17,1},{18,2},{19,3},{20,4},{21,5},{22,6},{23,7},{24,8},{25... | collective-permute-start | bytes 884744 | tf_op jit(solution)/shard_map/while/body/eval_jaxpr/ppermute | solution.py:24
  48.2 4.5 %collective-permute-start.1 = (f32[6,6,4,512]{3,2,1,0:T(4,128)S(1)}, f32[6,6,4,512]{3,2,1,0:T(4,128)S(1)}, u32[]{:S(2)}, u32[]{:S(2)}) collective-permute-start(f32[6,6,4,512]{3,2,1,0:T(4,128)S(1)} %get-tuple-element.357), channel_id=1, source_target_pairs={{0,16},{1,17},{2,18},{3,19},{4,20},{5,21},{6,22},{7,23},{8,24},{9,... | collective-permute-start | bytes 884744 | tf_op jit(solution)/shard_map/while/body/eval_jaxpr/ppermute | solution.py:21
  54.0 22.6 %collective-permute-start.2 = (f32[6,4,16,512]{3,2,1,0:T(8,128)}, f32[6,4,16,512]{3,2,1,0:T(8,128)}, u32[]{:S(2)}, u32[]{:S(2)}) collective-permute-start(f32[6,4,16,512]{3,2,1,0:T(8,128)} %get-tuple-element.358), channel_id=1, source_target_pairs={{1,0},{2,1},{3,2},{4,3},{5,4},{6,5},{7,6},{8,7},{9,8},{10,9},{11,1... | collective-permute-start | bytes 2359304 | tf_op jit(solution)/shard_map/while/body/eval_jaxpr/ppermute | solution.py:24
  55.3 36.0 %collective-permute-start.3 = (f32[6,4,16,512]{3,2,1,0:T(8,128)S(1)}, f32[6,4,16,512]{3,2,1,0:T(8,128)}, u32[]{:S(2)}, u32[]{:S(2)}) collective-permute-start(f32[6,4,16,512]{3,2,1,0:T(8,128)S(1)} %get-tuple-element.359), channel_id=1, source_target_pairs={{0,1},{1,2},{2,3},{3,4},{4,5},{5,6},{6,7},{7,8},{8,9},{9,10},{10,1... | collective-permute-start | bytes 2359304 | tf_op jit(solution)/shard_map/while/body/eval_jaxpr/ppermute | solution.py:21
  103.5 5.8 %collective-permute-start = (f32[6,6,4,512]{3,2,1,0:T(4,128)S(1)}, f32[6,6,4,512]{3,2,1,0:T(4,128)S(1)}, u32[]{:S(2)}, u32[]{:S(2)}) collective-permute-start(f32[6,6,4,512]{3,2,1,0:T(4,128)S(1)} %get-tuple-element.356), channel_id=1, source_target_pairs={{16,0},{17,1},{18,2},{19,3},{20,4},{21,5},{22,6},{23,7},{24,8},{25... | collective-permute-start | bytes 884744 | tf_op jit(solution)/shard_map/while/body/eval_jaxpr/ppermute | solution.py:24
  104.8 4.5 %collective-permute-start.1 = (f32[6,6,4,512]{3,2,1,0:T(4,128)S(1)}, f32[6,6,4,512]{3,2,1,0:T(4,128)S(1)}, u32[]{:S(2)}, u32[]{:S(2)}) collective-permute-start(f32[6,6,4,512]{3,2,1,0:T(4,128)S(1)} %get-tuple-element.357), channel_id=1, source_target_pairs={{0,16},{1,17},{2,18},{3,19},{4,20},{5,21},{6,22},{7,23},{8,24},{9,... | collective-permute-start | bytes 884744 | tf_op jit(solution)/shard_map/while/body/eval_jaxpr/ppermute | solution.py:21
  110.6 23.2 %collective-permute-start.2 = (f32[6,4,16,512]{3,2,1,0:T(8,128)}, f32[6,4,16,512]{3,2,1,0:T(8,128)}, u32[]{:S(2)}, u32[]{:S(2)}) collective-permute-start(f32[6,4,16,512]{3,2,1,0:T(8,128)} %get-tuple-element.358), channel_id=1, source_target_pairs={{1,0},{2,1},{3,2},{4,3},{5,4},{6,5},{7,6},{8,7},{9,8},{10,9},{11,1... | collective-permute-start | bytes 2359304 | tf_op jit(solution)/shard_map/while/body/eval_jaxpr/ppermute | solution.py:24
  111.9 39.0 %collective-permute-start.3 = (f32[6,4,16,512]{3,2,1,0:T(8,128)S(1)}, f32[6,4,16,512]{3,2,1,0:T(8,128)}, u32[]{:S(2)}, u32[]{:S(2)}) collective-permute-start(f32[6,4,16,512]{3,2,1,0:T(8,128)S(1)} %get-tuple-element.359), channel_id=1, source_target_pairs={{0,1},{1,2},{2,3},{3,4},{4,5},{5,6},{6,7},{7,8},{8,9},{9,10},{10,1... | collective-permute-start | bytes 2359304 | tf_op jit(solution)/shard_map/while/body/eval_jaxpr/ppermute | solution.py:21
  163.2 5.8 %collective-permute-start = (f32[6,6,4,512]{3,2,1,0:T(4,128)S(1)}, f32[6,6,4,512]{3,2,1,0:T(4,128)S(1)}, u32[]{:S(2)}, u32[]{:S(2)}) collective-permute-start(f32[6,6,4,512]{3,2,1,0:T(4,128)S(1)} %get-tuple-element.356), channel_id=1, source_target_pairs={{16,0},{17,1},{18,2},{19,3},{20,4},{21,5},{22,6},{23,7},{24,8},{25... | collective-permute-start | bytes 884744 | tf_op jit(solution)/shard_map/while/body/eval_jaxpr/ppermute | solution.py:24
  164.5 4.5 %collective-permute-start.1 = (f32[6,6,4,512]{3,2,1,0:T(4,128)S(1)}, f32[6,6,4,512]{3,2,1,0:T(4,128)S(1)}, u32[]{:S(2)}, u32[]{:S(2)}) collective-permute-start(f32[6,6,4,512]{3,2,1,0:T(4,128)S(1)} %get-tuple-element.357), channel_id=1, source_target_pairs={{0,16},{1,17},{2,18},{3,19},{4,20},{5,21},{6,22},{7,23},{8,24},{9,... | collective-permute-start | bytes 884744 | tf_op jit(solution)/shard_map/while/body/eval_jaxpr/ppermute | solution.py:21
  170.3 23.2 %collective-permute-start.2 = (f32[6,4,16,512]{3,2,1,0:T(8,128)}, f32[6,4,16,512]{3,2,1,0:T(8,128)}, u32[]{:S(2)}, u32[]{:S(2)}) collective-permute-start(f32[6,4,16,512]{3,2,1,0:T(8,128)} %get-tuple-element.358), channel_id=1, source_target_pairs={{1,0},{2,1},{3,2},{4,3},{5,4},{6,5},{7,6},{8,7},{9,8},{10,9},{11,1... | collective-permute-start | bytes 2359304 | tf_op jit(solution)/shard_map/while/body/eval_jaxpr/ppermute | solution.py:24
  171.6 37.4 %collective-permute-start.3 = (f32[6,4,16,512]{3,2,1,0:T(8,128)S(1)}, f32[6,4,16,512]{3,2,1,0:T(8,128)}, u32[]{:S(2)}, u32[]{:S(2)}) collective-permute-start(f32[6,4,16,512]{3,2,1,0:T(8,128)S(1)} %get-tuple-element.359), channel_id=1, source_target_pairs={{0,1},{1,2},{2,3},{3,4},{4,5},{5,6},{6,7},{7,8},{8,9},{9,10},{10,1... | collective-permute-start | bytes 2359304 | tf_op jit(solution)/shard_map/while/body/eval_jaxpr/ppermute | solution.py:21
  221.2 5.8 %collective-permute-start = (f32[6,6,4,512]{3,2,1,0:T(4,128)S(1)}, f32[6,6,4,512]{3,2,1,0:T(4,128)S(1)}, u32[]{:S(2)}, u32[]{:S(2)}) collective-permute-start(f32[6,6,4,512]{3,2,1,0:T(4,128)S(1)} %get-tuple-element.356), channel_id=1, source_target_pairs={{16,0},{17,1},{18,2},{19,3},{20,4},{21,5},{22,6},{23,7},{24,8},{25... | collective-permute-start | bytes 884744 | tf_op jit(solution)/shard_map/while/body/eval_jaxpr/ppermute | solution.py:24
  222.5 4.5 %collective-permute-start.1 = (f32[6,6,4,512]{3,2,1,0:T(4,128)S(1)}, f32[6,6,4,512]{3,2,1,0:T(4,128)S(1)}, u32[]{:S(2)}, u32[]{:S(2)}) collective-permute-start(f32[6,6,4,512]{3,2,1,0:T(4,128)S(1)} %get-tuple-element.357), channel_id=1, source_target_pairs={{0,16},{1,17},{2,18},{3,19},{4,20},{5,21},{6,22},{7,23},{8,24},{9,... | collective-permute-start | bytes 884744 | tf_op jit(solution)/shard_map/while/body/eval_jaxpr/ppermute | solution.py:21
  228.3 23.2 %collective-permute-start.2 = (f32[6,4,16,512]{3,2,1,0:T(8,128)}, f32[6,4,16,512]{3,2,1,0:T(8,128)}, u32[]{:S(2)}, u32[]{:S(2)}) collective-permute-start(f32[6,4,16,512]{3,2,1,0:T(8,128)} %get-tuple-element.358), channel_id=1, source_target_pairs={{1,0},{2,1},{3,2},{4,3},{5,4},{6,5},{7,6},{8,7},{9,8},{10,9},{11,1... | collective-permute-start | bytes 2359304 | tf_op jit(solution)/shard_map/while/body/eval_jaxpr/ppermute | solution.py:24
  229.6 39.0 %collective-permute-start.3 = (f32[6,4,16,512]{3,2,1,0:T(8,128)S(1)}, f32[6,4,16,512]{3,2,1,0:T(8,128)}, u32[]{:S(2)}, u32[]{:S(2)}) collective-permute-start(f32[6,4,16,512]{3,2,1,0:T(8,128)S(1)} %get-tuple-element.359), channel_id=1, source_target_pairs={{0,1},{1,2},{2,3},{3,4},{4,5},{5,6},{6,7},{7,8},{8,9},{9,10},{10,1... | collective-permute-start | bytes 2359304 | tf_op jit(solution)/shard_map/while/body/eval_jaxpr/ppermute | solution.py:21
  280.7 7.7 %copy-start = (f32[6,6,8,512]{3,2,1,0:T(8,128)}, f32[6,6,8,512]{3,2,1,0:T(8,128)S(1)}, u32[]{:S(2)}) copy-start(f32[6,6,8,512]{3,2,1,0:T(8,128)S(1)} %get-tuple-element.168) | copy-start | bytes 1769476
  280.7 6.4 %copy-start.4 = (f32[1,512,256]{2,1,0:T(8,128)S(1)}, f32[1,512,256]{2,1,0:T(8,128)}, u32[]{:S(2)}) copy-start(f32[1,512,256]{2,1,0:T(8,128)} %get-tuple-element.247) | copy-start | bytes 1572868
  280.7 6.4 %copy-start.5 = (f32[1,512,256]{2,1,0:T(8,128)S(1)}, f32[1,512,256]{2,1,0:T(8,128)}, u32[]{:S(2)}) copy-start(f32[1,512,256]{2,1,0:T(8,128)} %get-tuple-element.248) | copy-start | bytes 1572868
  280.7 7.0 %copy-start.2 = (f32[1,512,256]{2,1,0:T(8,128)S(1)}, f32[1,512,256]{2,1,0:T(8,128)}, u32[]{:S(2)}) copy-start(f32[1,512,256]{2,1,0:T(8,128)} %get-tuple-element.245) | copy-start | bytes 1572868
  280.8 7.0 %copy-start.3 = (f32[1,512,256]{2,1,0:T(8,128)S(1)}, f32[1,512,256]{2,1,0:T(8,128)}, u32[]{:S(2)}) copy-start(f32[1,512,256]{2,1,0:T(8,128)} %get-tuple-element.246) | copy-start | bytes 1572868
  280.9 7.6 %copy-start.8 = (f32[1,96,6]{1,2,0:T(8,128)S(1)}, f32[1,96,6]{1,2,0:T(8,128)}, u32[]{:S(2)}) copy-start(f32[1,96,6]{1,2,0:T(8,128)} %get-tuple-element.251) | copy-start | bytes 6916
  280.9 7.6 %copy-start.9 = (f32[1,96,6]{1,2,0:T(8,128)S(1)}, f32[1,96,6]{1,2,0:T(8,128)}, u32[]{:S(2)}) copy-start(f32[1,96,6]{1,2,0:T(8,128)} %get-tuple-element.252) | copy-start | bytes 6916
  283.4 6.1 %copy-start.6 = (f32[1,96,6]{1,2,0:T(8,128)S(1)}, f32[1,96,6]{1,2,0:T(8,128)}, u32[]{:S(2)}) copy-start(f32[1,96,6]{1,2,0:T(8,128)} %get-tuple-element.249) | copy-start | bytes 6916
  283.4 6.1 %copy-start.7 = (f32[1,96,6]{1,2,0:T(8,128)S(1)}, f32[1,96,6]{1,2,0:T(8,128)}, u32[]{:S(2)}) copy-start(f32[1,96,6]{1,2,0:T(8,128)} %get-tuple-element.250) | copy-start | bytes 6916
  289.5 2.6 copy-start.10
Sparse Core Ops, SparseCore 0:
  292.2 111.4 all-reduce.50
